TPU v7x, 512 devices: a whole 4x4x16 slice. The times are simulated.
512 devices in a mesh: segment: 16 (over z_lo, x), dp: 8 (over y, core), mp: 4 (over z_hi).
Axes of the slice: x: 4, y: 4, z: 16 (z_hi: 4, z_lo: 4; z = z_hi * 4 + z_lo), core: 2. Of those that a mesh axis runs over, the one named last changes fastest.
Arguments:
- encoder_image_states: bfloat16 [8, 128, 8192], P('dp', 'segment'), may hold values from -6 to 6
- frozen_key_value: bfloat16 [16, 8192, 2, 1024], P('segment', 'dp', None, 'mp'), may hold values from -0.0625 to 0.0625
- adapter_down_weight: bfloat16 [16, 8192, 128], P('segment', 'mp'), may hold values from -0.0625 to 0.0625
- adapter_up_weight: bfloat16 [16, 2, 64, 1024], P('segment', None, None, 'mp'), may hold values from -0.75 to 0.75
- queries: bfloat16 [16, 8, 128, 8192], P('segment', 'dp', None, 'mp'), may hold values from -9 to 9
- cotangent: bfloat16 [16, 8, 128, 8192], P('segment', 'dp', None, 'mp'), may hold values from -1.5 to 1.5
- text_token_length: int32 [8], P('dp'), may hold values from 32 to 128
- image_tile_count: int32 [8], P('dp'), may hold values from 1 to 4
Outputs:
- grad_down: bfloat16 [16, 8192, 128], P('segment', 'mp')
- up_gradient: bfloat16 [16, 2, 64, 1024], P('segment', None, None, 'mp')
- grad_image: float32 [8, 128, 8192], P('dp', 'segment')
All inputs are finite; a program needn't handle non-finite values.
Results may differ from a plain program's by a relative error of at most 0.017.
The roundings to bfloat16 on the way count: a program that leaves them out, or rounds other values in their place, can miss the bound.
Values may be sent and summed in bfloat16 or wider, within the bound.
No kernel may reach another device: no remote copies, remote signals or barrier semaphores. Data moves between devices by JAX's collectives and lax.ppermute only.
A program may use at most 64 MiB of HBM per device.

v0:
```python
import jax
import jax.numpy as jnp
from jax import lax
from jax.sharding import PartitionSpec as P

HD = 128
TILES = 4
adapter_scale = 2.0
contract_rows = (((0,), (0,)), ((), ()))
contracted_columns = (((1,), (1,)), ((), ()))


def body(
    encoder_image_states,
    frozen_key_value,
    adapter_down_weight,
    adapter_up_weight,
    queries,
    cotangent,
    text_token_length,
    image_tile_count,
):
    samples = encoder_image_states.shape[0]
    model_width = encoder_image_states.shape[2]
    whole_img = lax.all_gather(encoder_image_states, "segment", axis=1, tiled=True)
    image_rows = whole_img.shape[1]
    flat_rows = samples * image_rows
    flat_img = whole_img.reshape(flat_rows, model_width)
    fourth_part = adapter_down_weight.shape[1]
    parallel_index = lax.axis_index("mp")
    image_fourth = lax.dynamic_slice_in_dim(flat_img, parallel_index * fourth_part, fourth_part, 1)
    lowrank_state = adapter_up_weight.shape[2]
    key_value_columns = adapter_up_weight.shape[3]
    lowrank_projection = lax.psum(
        jnp.dot(image_fourth, adapter_down_weight[0], preferred_element_type=jnp.float32), "mp"
    ).astype(jnp.bfloat16)
    adapted_weight = jnp.concatenate(
        [
            jnp.dot(
                lowrank_projection[:, :lowrank_state],
                adapter_up_weight[0, 0],
                preferred_element_type=jnp.float32,
            ),
            jnp.dot(
                lowrank_projection[:, lowrank_state:],
                adapter_up_weight[0, 1],
                preferred_element_type=jnp.float32,
            ),
        ],
        axis=1,
    )
    local_weight = frozen_key_value[0]
    full_weight = lax.all_gather(local_weight, "dp", axis=0, tiled=True).reshape(
        model_width, 2 * key_value_columns
    )
    frozen_output = jnp.dot(flat_img, full_weight, preferred_element_type=jnp.float32)
    key_value_pair = (frozen_output + adapter_scale * adapted_weight).astype(jnp.bfloat16)
    local_heads = queries.shape[3] // HD
    local_kv = key_value_columns // HD
    group_size = local_heads // local_kv
    text_rows = queries.shape[2]
    query_rows = queries[0].reshape(samples, text_rows, local_kv, group_size, HD)
    cot_rows = cotangent[0].reshape(samples, text_rows, local_kv, group_size, HD)
    key_rows = key_value_pair[:, :key_value_columns].reshape(samples, image_rows, local_kv, HD)
    value_rows = key_value_pair[:, key_value_columns:].reshape(samples, image_rows, local_kv, HD)
    key_mask = jnp.arange(image_rows, dtype=jnp.int32)[None, :] < image_tile_count[:, None] * (
        image_rows // TILES
    )
    row_mask = (
        jnp.arange(text_rows, dtype=jnp.int32)[None, :] < text_token_length[:, None]
    ).astype(jnp.float32)
    scores = jnp.einsum(
        "btgrd,bjgd->bgrtj", query_rows, key_rows, preferred_element_type=jnp.float32
    ) * HD ** (-0.5)
    masked = jnp.where(key_mask[:, None, None, None, :], scores, -1e30)
    row_top = jnp.max(masked, axis=-1, keepdims=True)
    shifted = jnp.exp(masked - row_top)
    attention = shifted / jnp.sum(shifted, axis=-1, keepdims=True)
    row_gate = row_mask[:, None, None, :, None]
    kept = attention.astype(jnp.bfloat16) * row_gate.astype(jnp.bfloat16)
    dweights = jnp.einsum(
        "btgrd,bjgd->bgrtj", cot_rows, value_rows, preferred_element_type=jnp.float32
    )
    row_delta = jnp.sum(attention * dweights, axis=-1, keepdims=True)
    dscore = (attention * (dweights - row_delta) * row_gate * HD ** (-0.5)).astype(jnp.bfloat16)
    key_grad = jnp.einsum(
        "bgrtj,btgrd->bjgd", dscore, query_rows, preferred_element_type=jnp.float32
    )
    value_grad = jnp.einsum("bgrtj,btgrd->bjgd", kept, cot_rows, preferred_element_type=jnp.float32)
    kv_grad = jnp.concatenate(
        [
            key_grad.reshape(flat_rows, key_value_columns),
            value_grad.reshape(flat_rows, key_value_columns),
        ],
        axis=1,
    ).astype(jnp.bfloat16)
    backward_piece = adapter_scale * jnp.concatenate(
        [
            lax.dot_general(
                kv_grad[:, :key_value_columns],
                adapter_up_weight[0, 0],
                contracted_columns,
                preferred_element_type=jnp.float32,
            ),
            lax.dot_general(
                kv_grad[:, key_value_columns:],
                adapter_up_weight[0, 1],
                contracted_columns,
                preferred_element_type=jnp.float32,
            ),
        ],
        axis=1,
    )
    backward_lowrank = lax.psum(backward_piece, "mp").astype(jnp.bfloat16)
    up_gradient = adapter_scale * jnp.stack(
        [
            lax.dot_general(
                lowrank_projection[:, :lowrank_state],
                kv_grad[:, :key_value_columns],
                contract_rows,
                preferred_element_type=jnp.float32,
            ),
            lax.dot_general(
                lowrank_projection[:, lowrank_state:],
                kv_grad[:, key_value_columns:],
                contract_rows,
                preferred_element_type=jnp.float32,
            ),
        ]
    )
    grad_down = lax.dot_general(
        image_fourth, backward_lowrank, contract_rows, preferred_element_type=jnp.float32
    )
    down_sum, up_sum = lax.psum((grad_down, up_gradient), "dp")
    image_gradient_total = lax.dot_general(
        kv_grad, full_weight, contracted_columns, preferred_element_type=jnp.float32
    )
    adapter_portion = lax.dot_general(
        backward_lowrank,
        adapter_down_weight[0],
        contracted_columns,
        preferred_element_type=jnp.float32,
    )
    current_layer = lax.dynamic_slice_in_dim(
        image_gradient_total, parallel_index * fourth_part, fourth_part, 1
    )
    image_gradient_total = lax.dynamic_update_slice_in_dim(
        image_gradient_total, current_layer + adapter_portion, parallel_index * fourth_part, 1
    )
    image_gradient_total = image_gradient_total.reshape(samples, image_rows, model_width)
    shared_sum = lax.psum_scatter(image_gradient_total, "segment", scatter_dimension=1, tiled=True)
    result = lax.psum(shared_sum, "mp")
    return (down_sum.astype(jnp.bfloat16)[None], up_sum.astype(jnp.bfloat16)[None], result)


def solution(mesh):
    in_specs = (
        P("dp", "segment", None),
        P("segment", "dp", None, "mp"),
        P("segment", "mp", None),
        P("segment", None, None, "mp"),
        P("segment", "dp", None, "mp"),
        P("segment", "dp", None, "mp"),
        P("dp"),
        P("dp"),
    )
    out_specs = (P("segment", "mp", None), P("segment", None, None, "mp"), P("dp", "segment", None))
    return jax.shard_map(body, mesh=mesh, in_specs=in_specs, out_specs=out_specs, check_vma=False)
```

profile of v0, /device:TPU:2, one launch (start us, length us, event | category | flops | bytes accessed | tf_op | source)
XLA Modules:
  0.0 390.2 jit_solution(4577795114373816345)
XLA Ops:
  7.2 0.7 all-gather.4.cloned.1.call-update
  8.0 0.7 all-gather.6.cloned.1.call-update
  10.0 1.3 copy.38
  11.3 2.0 copy.39
  13.4 88.8 %all-gather.4.cloned.1.call-done = bf16[1,128,8192]{2,1,0:T(8,128)(2,1)} async-done(((bf16[1,8,8192]{2,1,0:T(8,128)(2,1)}), bf16[1,128,8192]{2,1,0:T(8,128)(2,1)}) %all-gather.4.cloned.1.call-update) | async-done | bytes 2097168 | tf_op jit(solution)/shard_map/all_gather | solution.py:25
  102.2 1.3 fusion.21
  103.6 25.9 %psum.35 = bf16[128,128]{1,0:T(8,128)(2,1)S(1)} all-reduce(f32[128,128]{1,0:T(8,128)S(1)} %fusion.21), channel_id=1, replica_groups=mesh['segment'=16,'dp'=8,'mp'=4] {'mp'}, use_global_device_ids=true, to_apply=%region_0.0 | all-reduce | flops 16384 | bytes 98304 | tf_op jit(solution)/shard_map/psum | solution.py:34
  129.5 0.2 fusion.42
  129.7 0.1 fusion.46
  129.8 30.6 %all-gather.6.cloned.1.call-done = bf16[1,8192,2,256]{3,2,0,1:T(2,128)(2,1)} async-done(((bf16[1,1024,2,256]{3,2,0,1:T(2,128)(2,1)}), bf16[1,8192,2,256]{3,2,0,1:T(2,128)(2,1)}) %all-gather.6.cloned.1.call-update) | async-done | bytes 8388624 | tf_op jit(solution)/shard_map/all_gather | solution.py:53
  160.5 8.2 %copy.40 = bf16[1024,8,2,256]{3,1,2,0:T(8,128)(2,1)} copy(bf16[1024,8,2,256]{3,2,1,0:T(2,128)(2,1)} %bitcast.113) | data formatting | bytes 16777216
  168.6 4.6 %fusion.10 = bf16[128,512]{1,0:T(8,128)(2,1)S(1)} fusion(bf16[8192,512]{1,0:T(8,128)(2,1)} %bitcast.108, bf16[1,128,8192]{2,1,0:T(8,128)(2,1)S(1)} %copy-done.1, f32[128,256]{1,0:T(8,128)S(1)} %fusion.42, f32[128,256]{1,0:T(8,128)S(1)} %fusion.46), kind=kOutput, calls=%fused_computation.11 | convolution fusion | flops 1074003968 | bytes 10878976 | tf_op jit(solution)/shard_map/dot_general | solution.py:56
  173.3 0.3 fusion.66
  173.6 0.2 fusion.16
  173.8 1.6 fusion.14
  175.4 0.1 fusion.40
  175.6 0.3 multiply_reduce_fusion
  175.9 0.5 fusion.13
  176.4 1.5 slice-done.1
  177.9 4.8 %fusion.34 = f32[128,8192]{1,0:T(8,128)} fusion(bf16[8192,512]{1,0:T(8,128)(2,1)S(1)} %bitcast.111, bf16[128,256]{0,1:T(8,128)(2,1)S(1)} %bitcast.118, bf16[128,256]{0,1:T(8,128)(2,1)S(1)} %bitcast.120), kind=kOutput, calls=%fused_computation.42 | convolution fusion | flops 1074003968 | bytes 12713984 | tf_op jit(solution)/shard_map/dot_general | solution.py:135
  182.7 0.1 fusion.44
  182.8 26.9 %psum.36 = bf16[128,128]{0,1:T(8,128)(2,1)S(1)} all-reduce(f32[128,128]{0,1:T(8,128)S(1)} %maximum_multiply_fusion.2), channel_id=1, replica_groups=mesh['segment'=16,'dp'=8,'mp'=4] {'mp'}, use_global_device_ids=true, to_apply=%region_4.5 | all-reduce | flops 16384 | bytes 98304 | tf_op jit(solution)/shard_map/psum | solution.py:114
  209.8 4.6 %copy.51 = f32[1,128,8192]{2,1,0:T(8,128)} copy(f32[1,128,8192]{2,1,0:T(8,128)} %bitcast.112) | data formatting | bytes 8388608
  214.3 2.5 fusion.1
  216.8 0.0 all-reduce.4.cloned.1.call-start
  216.9 1.3 fusion.23
  218.2 0.2 convolution_bitcast_fusion.3
  218.4 0.2 convolution_bitcast_fusion.4
  218.7 89.1 %reduce-scatter.2.cloned.1.call-done = f32[1,8,8192]{2,1,0:T(8,128)} async-done(((f32[1,128,8192]{2,1,0:T(8,128)}), f32[1,8,8192]{2,1,0:T(8,128)}) %reduce-scatter.2.cloned.1.call-update) | async-done | bytes 262160 | tf_op jit(solution)/shard_map/reduce_scatter | solution.py:151
  307.7 52.3 %all-reduce.5 = (bf16[2048,128]{1,0:T(8,128)(2,1)}, bf16[2,64,256]{2,1,0:T(8,128)(2,1)}) all-reduce(f32[2048,128]{1,0:T(8,128)} %fusion.23, f32[2,64,256]{2,1,0:T(8,128)S(1)} %maximum_multiply_fusion.1), channel_id=1, replica_groups=mesh['segment'=16,'dp'=8,'mp'=4] {'dp'}, use_global_device_ids=true, to_apply=%region_5.6 | all-reduce | flops 294912 | bytes 1769472 | tf_op jit(solution)/shard_map/psum | solution.py:134
  360.0 22.0 %all-reduce.4.cloned.1.call-done = f32[1,8,8192]{2,1,0:T(8,128)} async-done(((f32[1,8,8192]{2,1,0:T(8,128)}), f32[1,8,8192]{2,1,0:T(8,128)}) %all-reduce.4.cloned.1.call-update) | async-done | bytes 262160 | tf_op jit(solution)/shard_map/psum | solution.py:152
  382.0 1.7 copy.57
  (24 shorter events, 0.3 us)
Async XLA Ops:
  7.2 95.1 %copy-start = (bf16[1,2048,128]{2,1,0:T(8,128)(2,1)S(1)}, bf16[1,2048,128]{2,1,0:T(8,128)(2,1)}, u32[]{:S(2)}) copy-start(bf16[1,2048,128]{2,1,0:T(8,128)(2,1)} %param.10) | copy-start | bytes 1572868
  7.2 122.3 %copy-start.3 = (bf16[1,2,64,256]{3,2,1,0:T(8,128)(2,1)S(1)}, bf16[1,2,64,256]{3,2,1,0:T(8,128)(2,1)}, u32[]{:S(2)}) copy-start(bf16[1,2,64,256]{3,2,1,0:T(8,128)(2,1)} %param.11) | copy-start | bytes 196612
  7.2 95.0 %all-gather.4.cloned.1.call-start = ((), (), s32[]{:S(2)}) async-start(), calls=%async_computation.1 | async-start | bytes 2228224 | tf_op jit(solution)/shard_map/all_gather | solution.py:25
  7.9 152.5 %all-gather.6.cloned.1.call-start = ((), (), s32[]{:S(2)}) async-start(), calls=%async_computation.4 | async-start | bytes 9437184 | tf_op jit(solution)/shard_map/all_gather | solution.py:53
  8.7 299.0 %reduce-scatter.2.cloned.1.call-start = ((), (), s32[]{:S(2)}) async-start(), calls=%async_computation.2 | async-start | bytes 4456448 | tf_op jit(solution)/shard_map/reduce_scatter | solution.py:151
  160.5 8.2 %copy-start.1 = (bf16[1,128,8192]{2,1,0:T(8,128)(2,1)S(1)}, bf16[1,128,8192]{2,1,0:T(8,128)(2,1)}, u32[]{:S(2)}) copy-start(bf16[1,128,8192]{2,1,0:T(8,128)(2,1)} %all-gather.4.cloned.1.call-done) | copy-start | bytes 6291460
  173.3 2.2 copy-start.2
  173.8 2.6 slice-start
  175.6 2.4 slice-start.1
  216.8 165.2 %all-reduce.4.cloned.1.call-start = ((), (), s32[]{:S(2)}) async-start(), calls=%async_computation.3 | async-start | bytes 524288 | tf_op jit(solution)/shard_map/psum | solution.py:152
Sparse Core Ops, SparseCore 0:
  10.1 92.1 all-gather.3
  104.4 56.0 all-gather.5
  217.0 90.7 reduce-scatter.1
  310.5 71.4 all-reduce.3
where the time goes:
time: 391 us; the launch traced here: 390 us
  waiting for transfers between devices  232 us (59%)
  blocking collectives  105 us (27%)
  local copies, waits for them, and re-layouts  19.3 us (5%)
  matrix products  18.3 us (5%)
  between operations  15.2 us (4%)
    reduce_scatter x1, waiting for transfers between devices, body(): lax.psum_scatter(image_gradient_total, 'segment', scatter_dimension=1, ti...  89.1 us
    all_gather x1, waiting for transfers between devices, body(): lax.all_gather(encoder_image_states, 'segment', axis=1, tiled=True)  88.8 us
    psum x1, blocking collectives, body(): down_sum, up_sum = lax.psum((grad_down, up_gradient), 'dp')  52.3 us
    all_gather x1, waiting for transfers between devices, body(): lax.all_gather(local_weight, 'dp', axis=0, tiled=True)  30.6 us
    psum x1, blocking collectives, body(): backward_lowrank = lax.psum(backward_piece, 'mp').astype(jnp.bfloat16)  26.9 us
    psum x1, blocking collectives, body(): lax.psum(jnp.dot(image_fourth, adapter_down_weight[0], preferred_element_...  25.9 us
    psum x1, waiting for transfers between devices, body(): result = lax.psum(shared_sum, 'mp')  22 us
    unnamed x15, local copies, waits for them, and re-layouts  15.9 us
  transfers between devices with their start and end apart: 4, of which 4 were waited for; matrix products, arithmetic and copies ran while one was open for 2% of the time, Pallas kernels for 0%

commit v1 on v0

--- a/solution.py
+++ b/solution.py
@@ -22,7 +22,12 @@
 ):
     samples = encoder_image_states.shape[0]
     model_width = encoder_image_states.shape[2]
-    whole_img = lax.all_gather(encoder_image_states, "segment", axis=1, tiled=True)
+    whole_img = jnp.concatenate(
+        lax.all_to_all(
+            jnp.stack([encoder_image_states] * lax.axis_size("segment")), "segment", 0, 0
+        ),
+        axis=1,
+    )
     image_rows = whole_img.shape[1]
     flat_rows = samples * image_rows
     flat_img = whole_img.reshape(flat_rows, model_width)

time: 391 us -> 324 us (0.83)
  waiting for transfers between devices: 232 us -> 155 us
  starting transfers between devices: 0.16 us -> 9.63 us
    all_gather x1 -> x0, waiting for transfers between devices: 88.8 us -> none  [body(): lax.all_gather(encoder_image_states, 'segment', axis=1, tiled=True)]
    all_to_all x0 -> x1, waiting for transfers between devices: none -> 36.1 us  [body(): lax.all_to_all(jnp.stack([encoder_image_states] * lax.axis_size('segment'...]
    all_gather x1, waiting for transfers between devices: 30.6 us -> 0.02 us  [body(): lax.all_gather(local_weight, 'dp', axis=0, tiled=True)]
    all_to_all x0 -> x1, starting transfers between devices: none -> 9.52 us  [body(): lax.all_to_all(jnp.stack([encoder_image_states] * lax.axis_size('segment'...]
    reduce_scatter x1, waiting for transfers between devices: 89.1 us -> 96.1 us  [body(): lax.psum_scatter(image_gradient_total, 'segment', scatter_dimension=1, ti...]
    unnamed x15 -> x13, local copies, waits for them, and re-layouts: 15.9 us -> 15.7 us
  transfers between devices with their start and end apart: 4 -> 4, of which waited for: 4 -> 3; matrix products, arithmetic and copies ran while one was open for 2% -> 3% of each run, Pallas kernels for 0% -> 0%
where the time goes in v1:
time: 324 us; the launch traced here: 323 us
  waiting for transfers between devices  155 us (48%)
  blocking collectives  104 us (32%)
  local copies, waits for them, and re-layouts  21.6 us (7%)
  matrix products  17.4 us (5%)
  between operations  15.2 us (5%)
  starting transfers between devices  9.63 us (3%)
    reduce_scatter x1, waiting for transfers between devices, body(): lax.psum_scatter(image_gradient_total, 'segment', scatter_dimension=1, ti...  96.1 us
    psum x1, blocking collectives, body(): down_sum, up_sum = lax.psum((grad_down, up_gradient), 'dp')  52.3 us
    all_to_all x1, waiting for transfers between devices, body(): lax.all_to_all(jnp.stack([encoder_image_states] * lax.axis_size('segment'...  36.1 us
    psum x1, blocking collectives, body(): lax.psum(jnp.dot(image_fourth, adapter_down_weight[0], preferred_element_...  28.4 us
    psum x1, blocking collectives, body(): backward_lowrank = lax.psum(backward_piece, 'mp').astype(jnp.bfloat16)  23.7 us
    psum x1, waiting for transfers between devices, body(): result = lax.psum(shared_sum, 'mp')  22 us
    unnamed x13, local copies, waits for them, and re-layouts  15.7 us
    all_to_all x1, starting transfers between devices, body(): lax.all_to_all(jnp.stack([encoder_image_states] * lax.axis_size('segment'...  9.52 us
  transfers between devices with their start and end apart: 4, of which 3 were waited for; matrix products, arithmetic and copies ran while one was open for 3% of the time, Pallas kernels for 0%

profile of v1, /device:TPU:2, one launch (start us, length us, event | category | flops | bytes accessed | tf_op | source)
XLA Modules:
  0.0 323.4 jit_solution(5856999373383504148)
XLA Ops:
  7.2 0.7 all-gather.3.cloned.1.call-update
  7.9 2.5 stack.8
  10.4 9.5 %all-to-all-start = ((bf16[16,1,8,8192]{3,2,1,0:T(8,128)(2,1)}), bf16[16,1,8,8192]{3,2,1,0:T(8,128)(2,1)S(1)}, u32[]{:S(2)}, u32[]{:S(2)}) async-start(bf16[16,1,8,8192]{3,2,1,0:T(8,128)(2,1)} %stack.8), calls=%async_computation | async-start | bytes 4194304 | tf_op jit(solution)/shard_map/all_to_all | solution.py:26
  21.3 1.3 copy.38
  22.6 2.0 copy.39
  24.7 36.1 %all-to-all-done = bf16[16,1,8,8192]{3,2,1,0:T(8,128)(2,1)S(1)} async-done(((bf16[16,1,8,8192]{3,2,1,0:T(8,128)(2,1)}), bf16[16,1,8,8192]{3,2,1,0:T(8,128)(2,1)S(1)}, u32[]{:S(2)}, u32[]{:S(2)}) %all-to-all-start) | async-done | bytes 2097184 | tf_op jit(solution)/shard_map/all_to_all | solution.py:26
  60.7 0.3 fusion.14
  61.0 28.4 %psum.35 = bf16[128,128]{1,0:T(8,128)(2,1)S(1)} all-reduce(f32[128,128]{1,0:T(8,128)S(1)} %fusion.14), channel_id=1, replica_groups=mesh['segment'=16,'dp'=8,'mp'=4] {'mp'}, use_global_device_ids=true, to_apply=%region_0.0 | all-reduce | flops 16384 | bytes 98304 | tf_op jit(solution)/shard_map/psum | solution.py:39
  89.5 0.2 fusion.33
  89.7 0.1 fusion.37
  89.9 8.0 %copy.40 = bf16[1024,8,2,256]{3,1,2,0:T(8,128)(2,1)} copy(bf16[1024,8,2,256]{3,2,1,0:T(2,128)(2,1)} %bitcast.107) | data formatting | bytes 16777216
  97.9 4.6 %fusion.5 = bf16[128,512]{1,0:T(8,128)(2,1)S(1)} fusion(bf16[8192,512]{1,0:T(8,128)(2,1)} %bitcast.100, f32[128,256]{1,0:T(8,128)S(1)} %fusion.33, f32[128,256]{1,0:T(8,128)S(1)} %fusion.37, bf16[16,1,8,8192]{3,2,1,0:T(8,128)(2,1)S(1)} %all-to-all-done), kind=kOutput, calls=%fused_computation.9 | convolution fusion | flops 1074003968 | bytes 10878976 | tf_op jit(solution)/shard_map/dot_general | solution.py:61
  102.6 0.3 fusion.58
  102.9 0.2 fusion.9
  103.1 1.6 fusion.7
  104.7 0.1 fusion.31
  104.8 0.3 multiply_reduce_fusion
  105.2 0.5 fusion.6
  105.7 1.4 slice-done.1
  107.2 4.8 %fusion.25 = f32[128,8192]{1,0:T(8,128)} fusion(bf16[8192,512]{1,0:T(8,128)(2,1)S(1)} %bitcast.103, bf16[128,256]{0,1:T(8,128)(2,1)S(1)} %bitcast.112, bf16[128,256]{0,1:T(8,128)(2,1)S(1)} %bitcast.114), kind=kOutput, calls=%fused_computation.38 | convolution fusion | flops 1074003968 | bytes 12713984 | tf_op jit(solution)/shard_map/dot_general | solution.py:140
  111.9 0.1 fusion.35
  112.1 23.7 %psum.36 = bf16[128,128]{0,1:T(8,128)(2,1)S(1)} all-reduce(f32[128,128]{0,1:T(8,128)S(1)} %maximum_multiply_fusion.2), channel_id=1, replica_groups=mesh['segment'=16,'dp'=8,'mp'=4] {'mp'}, use_global_device_ids=true, to_apply=%region_4.5 | all-reduce | flops 16384 | bytes 98304 | tf_op jit(solution)/shard_map/psum | solution.py:119
  135.8 4.6 %copy.51 = f32[1,128,8192]{2,1,0:T(8,128)} copy(f32[1,128,8192]{2,1,0:T(8,128)} %bitcast.106) | data formatting | bytes 8388608
  140.3 2.6 fusion.1
  142.9 0.0 all-reduce.4.cloned.1.call-start
  143.0 1.3 fusion.21
  144.3 0.2 convolution_bitcast_fusion.3
  144.5 0.2 convolution_bitcast_fusion.4
  144.8 96.1 %reduce-scatter.2.cloned.1.call-done = f32[1,8,8192]{2,1,0:T(8,128)} async-done(((f32[1,128,8192]{2,1,0:T(8,128)}), f32[1,8,8192]{2,1,0:T(8,128)}) %reduce-scatter.2.cloned.1.call-update) | async-done | bytes 262160 | tf_op jit(solution)/shard_map/reduce_scatter | solution.py:156
  240.9 52.3 %all-reduce.5 = (bf16[2048,128]{1,0:T(8,128)(2,1)}, bf16[2,64,256]{2,1,0:T(8,128)(2,1)}) all-reduce(f32[2048,128]{1,0:T(8,128)} %fusion.21, f32[2,64,256]{2,1,0:T(8,128)S(1)} %maximum_multiply_fusion.1), channel_id=1, replica_groups=mesh['segment'=16,'dp'=8,'mp'=4] {'dp'}, use_global_device_ids=true, to_apply=%region_5.6 | all-reduce | flops 294912 | bytes 1769472 | tf_op jit(solution)/shard_map/psum | solution.py:139
  293.2 22.0 %all-reduce.4.cloned.1.call-done = f32[1,8,8192]{2,1,0:T(8,128)} async-done(((f32[1,8,8192]{2,1,0:T(8,128)}), f32[1,8,8192]{2,1,0:T(8,128)}) %all-reduce.4.cloned.1.call-update) | async-done | bytes 262160 | tf_op jit(solution)/shard_map/psum | solution.py:157
  315.2 1.7 copy.57
  (22 shorter events, 0.3 us)
Async XLA Ops:
  7.2 53.6 %copy-start = (bf16[1,2048,128]{2,1,0:T(8,128)(2,1)S(1)}, bf16[1,2048,128]{2,1,0:T(8,128)(2,1)}, u32[]{:S(2)}) copy-start(bf16[1,2048,128]{2,1,0:T(8,128)(2,1)} %param.10) | copy-start | bytes 1572868
  7.2 82.7 %all-gather.3.cloned.1.call-start = ((), (), s32[]{:S(2)}) async-start(), calls=%async_computation.4 | async-start | bytes 9437184 | tf_op jit(solution)/shard_map/all_gather | solution.py:58
  10.4 79.1 %copy-start.2 = (bf16[1,2,64,256]{3,2,1,0:T(8,128)(2,1)S(1)}, bf16[1,2,64,256]{3,2,1,0:T(8,128)(2,1)}, u32[]{:S(2)}) copy-start(bf16[1,2,64,256]{3,2,1,0:T(8,128)(2,1)} %param.11) | copy-start | bytes 196612
  10.4 50.3 %all-to-all-start = ((bf16[16,1,8,8192]{3,2,1,0:T(8,128)(2,1)}), bf16[16,1,8,8192]{3,2,1,0:T(8,128)(2,1)S(1)}, u32[]{:S(2)}, u32[]{:S(2)}) async-start(bf16[16,1,8,8192]{3,2,1,0:T(8,128)(2,1)} %stack.8), calls=%async_computation | async-start | bytes 4194304 | tf_op jit(solution)/shard_map/all_to_all | solution.py:26
  19.9 220.9 %reduce-scatter.2.cloned.1.call-start = ((), (), s32[]{:S(2)}) async-start(), calls=%async_computation.2 | async-start | bytes 4456448 | tf_op jit(solution)/shard_map/reduce_scatter | solution.py:156
  102.6 2.2 copy-start.1
  103.1 2.7 slice-start
  104.8 2.4 slice-start.1
  142.9 172.3 %all-reduce.4.cloned.1.call-start = ((), (), s32[]{:S(2)}) async-start(), calls=%async_computation.3 | async-start | bytes 524288 | tf_op jit(solution)/shard_map/psum | solution.py:157
Sparse Core Ops, SparseCore 0:
  10.1 61.7 all-gather.2
  143.0 97.7 reduce-scatter.1
  243.8 71.3 all-reduce.3
